TPU v7x, 128 devices: a whole 4x4x4 slice. The times are simulated.
128 devices in a mesh: seq: 32 (over z_lo, y, x), fsdp: 4 (over z_hi, core).
Axes of the slice: x: 4, y: 4, z: 4 (z_hi: 2, z_lo: 2; z = z_hi * 2 + z_lo), core: 2. Of those that a mesh axis runs over, the one named last changes fastest.
Arguments:
- tokens: bfloat16 [4, 8192, 2048], P('fsdp', 'seq'), may hold values from -6 to 6
- w_in: bfloat16 [2048, 2304], P('fsdp'), may hold values from -0.125 to 0.125
- log_decay: float32 [4, 32, 8192], P('fsdp', None, 'seq'), may hold values from -2 to 0, as said below
- grad_out: bfloat16 [4, 8192, 2048], P('fsdp', 'seq'), may hold values from -6 to 6
Outputs:
- mixer_out: bfloat16 [4, 8192, 2048], P('fsdp', 'seq')
- grad_tokens: bfloat16 [4, 8192, 2048], P('fsdp', 'seq')
- grad_weights: float32 [2048, 2304], P(('seq', 'fsdp'))
Inputs may be any that keep to these rules, and one draw needn't show every extreme that they name: `log_decay`: each entry is the logarithm of a decay factor below one.
All inputs are finite; a program needn't handle non-finite values.
Results may differ from a plain program's by a relative error of at most 0.015.
Values may be sent and summed in bfloat16 or wider, within the bound.
A program may use at most 192 MiB of HBM per device.

v0:
```python
import jax
import jax.numpy as jnp
from jax import lax
from jax.sharding import PartitionSpec as P

BLOCK = 256
highest = lax.Precision.HIGHEST
epsilon = 1e-05


def entering_2(shard, axis, join, neutral, backward):
    count = lax.axis_size(axis)
    place = lax.axis_index(axis)
    ahead = count - 1 - place if backward else place
    gathered = jax.tree.map(
        lambda a, kind: lax.all_gather(a.astype(kind), axis), shard, (jnp.bfloat16, jnp.bfloat16)
    )
    state = jax.tree.map(lambda a, e: jnp.zeros_like(a) + jnp.asarray(e, a.dtype), shard, neutral)

    def one(step, state):
        source = count - 1 - step if backward else step
        return join(
            state,
            jax.tree.map(
                lambda a, own: lax.dynamic_index_in_dim(a, source, 0, False).astype(own.dtype),
                gathered,
                shard,
            ),
        )

    return lax.fori_loop(0, ahead, one, state)


def combine_states(earlier, latter):
    return (earlier[0] + latter[0], jnp.exp(latter[0])[:, None, None] * earlier[1] + latter[1])


def block_chain(log_rates, terms, backward, start_state):

    def advance(carried, packed):
        log_k, term_k = packed
        return (jnp.exp(log_k)[:, None, None] * carried + term_k, carried)

    finish, inputs = lax.scan(advance, start_state, (log_rates, terms), reverse=backward)
    return (inputs, finish)


def decay_matrix(cumulative, log_rates):
    extent = cumulative.shape[-1]
    row_idx = lax.broadcasted_iota(jnp.int32, (extent, extent), 0)
    col_idx = lax.broadcasted_iota(jnp.int32, (extent, extent), 1)
    later_gap = cumulative[:, :, None] - cumulative[:, None, :]
    exclusive = cumulative - log_rates
    earlier_gap = exclusive[:, None, :] - exclusive[:, :, None]
    exponent = jnp.where(
        row_idx > col_idx, later_gap, jnp.where(row_idx < col_idx, earlier_gap, 0.0)
    )
    return jnp.exp(exponent) + (row_idx == col_idx).astype(jnp.float32)


def to_groups(array, axis, per_group):
    extents = array.shape
    grouped_shape = extents[:axis] + (extents[axis] // per_group, per_group) + extents[axis + 1 :]
    return jnp.moveaxis(array.reshape(grouped_shape), axis, 0)


def from_groups(array, axis):
    moved = jnp.moveaxis(array, 0, axis)
    extents = moved.shape
    return moved.reshape(
        extents[:axis] + (extents[axis] * extents[axis + 1],) + extents[axis + 2 :]
    )


def on_device(tokens, w_in, log_decay, grad_out):
    local_tokens = tokens[0]
    log_rates = log_decay[0]
    upstream_grad = grad_out[0]
    token_count = local_tokens.shape[0]
    hidden_width = local_tokens.shape[1]
    head_count = log_rates.shape[0]
    col_count = w_in.shape[1]
    inner_width = upstream_grad.shape[1]
    head_size = inner_width // head_count
    state_size = (col_count - inner_width) // 2
    block_count = token_count // BLOCK
    per_group = 8
    projected = jnp.dot(
        local_tokens,
        lax.all_gather(w_in, "fsdp", axis=0, tiled=True),
        preferred_element_type=jnp.float32,
    )
    xbc_rows = projected.astype(jnp.bfloat16)
    xbc_rows = lax.optimization_barrier(xbc_rows)
    xbc_float = xbc_rows.astype(jnp.float32)
    values = xbc_float[:, :inner_width].reshape(block_count, BLOCK, head_count, head_size)
    key_rows = xbc_float[:, inner_width : inner_width + state_size].reshape(
        block_count, BLOCK, state_size
    )
    queries = xbc_float[:, inner_width + state_size :].reshape(block_count, BLOCK, state_size)
    key_half = xbc_rows[:, inner_width : inner_width + state_size].reshape(
        block_count, BLOCK, state_size
    )
    query_half = xbc_rows[:, inner_width + state_size :].reshape(block_count, BLOCK, state_size)
    blocked = log_rates.reshape(head_count, block_count, BLOCK).transpose(1, 0, 2)
    cumulative = jnp.cumsum(blocked, axis=-1)
    totals = cumulative[:, :, -1]
    to_end = jnp.exp(totals[:, :, None] - cumulative)
    from_start = jnp.exp(cumulative - blocked)
    enter_weight = jnp.exp(cumulative)
    leave_weight = jnp.exp(totals[:, :, None] - (cumulative - blocked))
    end_terms = jnp.einsum("khq,kqhp,kqn->khpn", to_end, values, key_rows, precision=highest)
    start_terms = jnp.einsum("khq,kqhp,kqn->khpn", from_start, values, key_rows, precision=highest)
    zero_state = jnp.zeros((head_count, head_size, state_size), jnp.float32)
    none_log = jnp.zeros((head_count,), jnp.float32)
    device_log = jnp.sum(totals, axis=0)
    _, end_total = block_chain(totals, end_terms, False, zero_state)
    _, start_total = block_chain(totals, start_terms, True, zero_state)
    entering = entering_2(
        (device_log, end_total), "seq", combine_states, (none_log, zero_state), False
    )[1]
    arriving = entering_2(
        (device_log, start_total), "seq", combine_states, (none_log, zero_state), True
    )[1]
    fwd_in, _ = block_chain(totals, end_terms, False, entering)
    rev_next, _ = block_chain(totals, start_terms, True, arriving)

    def block_forward(packed):
        (
            block_vals,
            block_khalf,
            block_qhalf,
            block_queries,
            block_cumul,
            block_logs,
            block_enter,
            block_leave,
            state_in,
            state_next,
        ) = packed
        affinity = lax.dot_general(
            block_qhalf, block_khalf, (((1,), (1,)), ((), ())), preferred_element_type=jnp.float32
        )

        def group_forward(section):
            group_values, group_cumul, group_logs = section
            weighted = affinity[None] * decay_matrix(group_cumul, group_logs)
            return jnp.einsum("gij,jgp->igp", weighted, group_values, precision=highest)

        group_parts = lax.map(
            group_forward,
            (
                to_groups(block_vals, 1, per_group),
                to_groups(block_cumul, 0, per_group),
                to_groups(block_logs, 0, per_group),
            ),
        )
        inner_part = from_groups(group_parts, 1)
        carried_in = (
            jnp.einsum("qn,hpn->qhp", block_queries, state_in, precision=highest)
            * block_enter.T[:, :, None]
        )
        carried_back = (
            jnp.einsum("qn,hpn->qhp", block_queries, state_next, precision=highest)
            * block_leave.T[:, :, None]
        )
        return inner_part + carried_in + carried_back

    mixture = lax.map(
        block_forward,
        (
            values,
            key_half,
            query_half,
            queries,
            cumulative,
            blocked,
            enter_weight,
            leave_weight,
            fwd_in,
            rev_next,
        ),
    )
    row_scale = jnp.sqrt(jnp.mean(mixture * mixture, axis=-1) + epsilon)
    normed = mixture / row_scale[..., None]
    mixer_out = normed.astype(jnp.bfloat16).reshape(1, token_count, inner_width)
    upstream = upstream_grad.astype(jnp.float32).reshape(block_count, BLOCK, head_count, head_size)
    grad_mixture = (
        upstream - normed * jnp.mean(upstream * normed, axis=-1, keepdims=True)
    ) / row_scale[..., None]
    in_adjoint = jnp.einsum(
        "khq,kqhp,kqn->khpn", enter_weight, grad_mixture, queries, precision=highest
    )
    out_adjoint = jnp.einsum(
        "khq,kqhp,kqn->khpn", leave_weight, grad_mixture, queries, precision=highest
    )
    _, in_total = block_chain(totals, in_adjoint, True, zero_state)
    _, out_total = block_chain(totals, out_adjoint, False, zero_state)
    later_adjoint = entering_2(
        (device_log, in_total), "seq", combine_states, (none_log, zero_state), True
    )[1]
    earlier_adjoint = entering_2(
        (device_log, out_total), "seq", combine_states, (none_log, zero_state), False
    )[1]
    grad_ends, _ = block_chain(totals, in_adjoint, True, later_adjoint)
    grad_starts, _ = block_chain(totals, out_adjoint, False, earlier_adjoint)

    def block_backward(packed):
        (
            block_vals,
            block_keys,
            block_queries,
            block_khalf,
            block_qhalf,
            block_cumul,
            block_logs,
            block_enter,
            block_leave,
            block_end,
            block_start,
            state_in,
            state_next,
            block_grad,
            block_grad_end,
            block_grad_start,
        ) = packed
        affinity = lax.dot_general(
            block_qhalf, block_khalf, (((1,), (1,)), ((), ())), preferred_element_type=jnp.float32
        )

        def group_backward(section):
            group_values, group_cumul, group_logs, group_grad = section
            decays = decay_matrix(group_cumul, group_logs)
            weighted = affinity[None] * decays
            grad_vals = jnp.einsum("gij,igp->jgp", weighted, group_grad, precision=highest)
            grad_weighted = jnp.einsum("igp,jgp->gij", group_grad, group_values, precision=highest)
            return (grad_vals, jnp.sum(grad_weighted * decays, axis=0))

        group_vals, group_affinity = lax.map(
            group_backward,
            (
                to_groups(block_vals, 1, per_group),
                to_groups(block_cumul, 0, per_group),
                to_groups(block_logs, 0, per_group),
                to_groups(block_grad, 1, per_group),
            ),
        )
        grad_affinity = jnp.sum(group_affinity, axis=0)
        enter_cols = block_enter.T[:, :, None]
        leave_cols = block_leave.T[:, :, None]
        end_cols = block_end.T[:, :, None]
        start_cols = block_start.T[:, :, None]
        grad_queries = jnp.dot(grad_affinity, block_keys, precision=highest)
        grad_queries = grad_queries + jnp.einsum(
            "qhp,hpn->qn", block_grad * enter_cols, state_in, precision=highest
        )
        grad_queries = grad_queries + jnp.einsum(
            "qhp,hpn->qn", block_grad * leave_cols, state_next, precision=highest
        )
        grad_keys = jnp.dot(grad_affinity.T, block_queries, precision=highest)
        grad_keys = grad_keys + jnp.einsum(
            "qhp,hpn->qn", block_vals * end_cols, block_grad_end, precision=highest
        )
        grad_keys = grad_keys + jnp.einsum(
            "qhp,hpn->qn", block_vals * start_cols, block_grad_start, precision=highest
        )
        grad_values = from_groups(group_vals, 1)
        grad_values = grad_values + end_cols * jnp.einsum(
            "qn,hpn->qhp", block_keys, block_grad_end, precision=highest
        )
        grad_values = grad_values + start_cols * jnp.einsum(
            "qn,hpn->qhp", block_keys, block_grad_start, precision=highest
        )
        return (grad_values, grad_keys, grad_queries)

    grad_values, grad_keys, grad_queries = lax.map(
        block_backward,
        (
            values,
            key_rows,
            queries,
            key_half,
            query_half,
            cumulative,
            blocked,
            enter_weight,
            leave_weight,
            to_end,
            from_start,
            fwd_in,
            rev_next,
            grad_mixture,
            grad_ends,
            grad_starts,
        ),
    )
    grad_proj = jnp.concatenate(
        [
            grad_values.reshape(token_count, inner_width),
            grad_keys.reshape(token_count, state_size),
            grad_queries.reshape(token_count, state_size),
        ],
        axis=1,
    ).astype(jnp.bfloat16)
    grad_local = lax.dot_general(
        grad_proj,
        lax.all_gather(w_in, "fsdp", axis=0, tiled=True),
        (((1,), (1,)), ((), ())),
        preferred_element_type=jnp.float32,
    )
    grad_tokens = grad_local.astype(jnp.bfloat16).reshape(1, token_count, hidden_width)
    grad_weights = lax.psum_scatter(
        lax.dot_general(
            local_tokens, grad_proj, (((0,), (0,)), ((), ())), preferred_element_type=jnp.float32
        ),
        ("seq", "fsdp"),
        scatter_dimension=0,
        tiled=True,
    )
    return (mixer_out, grad_tokens, grad_weights)


def solution(mesh):
    return jax.shard_map(
        on_device,
        mesh=mesh,
        in_specs=(
            P("fsdp", "seq", None),
            P("fsdp", None),
            P("fsdp", None, "seq"),
            P("fsdp", "seq", None),
        ),
        out_specs=(P("fsdp", "seq", None), P("fsdp", "seq", None), P(("seq", "fsdp"), None)),
        check_vma=False,
    )
```

profile of v0, /device:TPU:0, one launch (start us, length us, event | category | flops | bytes accessed | tf_op | source)
XLA Modules:
  0.0 1677.7 jit_solution(10138005019356209090)
XLA Ops:
  9.2 71.4 %all-gather.11.cloned.1.call-done = bf16[2048,2304]{1,0:T(8,128)(2,1)} async-done(((bf16[512,2304]{1,0:T(8,128)(2,1)}), bf16[2048,2304]{1,0:T(8,128)(2,1)}) %all-gather.11.cloned.1.call-update) | async-done | bytes 9437200 | tf_op jit(solution)/shard_map/all_gather | solution.py:90
  80.6 6.3 convolution_convert_fusion
  103.1 81.3 %all-gather = bf16[32,32,1]{1,2,0:T(2,128)(2,1)S(1)} all-gather(bf16[1,32,1]{1,2,0:T(2,128)(2,1)S(1)} %slice.83), channel_id=2, replica_groups=mesh['seq'=32,'fsdp'=4] {'seq'}, dimensions={0}, use_global_device_ids=true | all-gather | bytes 2112 | tf_op jit(solution)/shard_map/all_gather | solution.py:16
  190.4 18.2 %while.56 = (s32[]{:T(128)}, f32[4,256,8,64]{1,3,2,0:T(8,128)}, f32[4,256,8,64]{1,3,2,0:T(8,128)S(1)}, f32[256,256]{1,0:T(8,128)}, f32[4,8,256]{2,1,0:T(8,128)S(1)}, /*index=5*/f32[4,8,256]{2,1,0:T(8,128)S(1)}, s32[]{:T(128)}) while((s32[]{:T(128)}, f32[4,256,8,64]{1,3,2,0:T(8,128)}, f32[4,256,8,64]{1,3,2,0:T(8,128)S(1)}, ...), condition=%wide.region_3.4_spmd, body=%wide.region_2.3_spmd.sunk | while | flops 406063104 | bytes 2171997 | solution.py:150
  190.4 4.5 fusion.177
  195.0 4.5 fusion.177
  199.6 4.5 fusion.177
  204.1 4.5 fusion.177
  208.6 76.7 %all-gather.15.cloned.1.call-done = bf16[1024,64,128]{2,1,0:T(8,128)(2,1)} async-done(((bf16[32,64,128]{2,1,0:T(8,128)(2,1)}), bf16[1024,64,128]{2,1,0:T(8,128)(2,1)}) %all-gather.15.cloned.1.call-update) | async-done | bytes 16777232 | tf_op jit(solution)/shard_map/all_gather | solution.py:16
  285.4 41.9 %while.58 = (s32[]{:T(128)}, f32[32,64,128]{2,1,0:T(8,128)S(1)}, s32[]{:T(128)}, bf16[32,32]{1,0:T(8,128)(2,1)S(1)}, bf16[32,32,64,128]{3,2,1,0:T(8,128)(2,1)}, ...) while((s32[]{:T(128)}, f32[32,64,128]{2,1,0:T(8,128)S(1)}, s32[]{:T(128)}, bf16[32,32]{1,0:T(8,128)(2,1)S(1)}, ...), condition=%wide.region_7.8_spmd, body=%wide.region_6.7_spmd.sunk | while | flops 786470 | bytes 2621915 | solution.py:31
  327.3 149.6 %all-gather.13.cloned.1.call-done = bf16[1024,64,128]{2,1,0:T(8,128)(2,1)} async-done(((bf16[32,64,128]{2,1,0:T(8,128)(2,1)}), bf16[1024,64,128]{2,1,0:T(8,128)(2,1)}) %all-gather.13.cloned.1.call-update) | async-done | bytes 16777232 | tf_op jit(solution)/shard_map/all_gather | solution.py:16
  488.3 3.5 fusion.87
  493.6 35.1 %while.59 = (s32[]{:T(128)}, f32[4,256,8,64]{1,3,2,0:T(8,128)}, f32[4,256,256]{2,1,0:T(8,128)}, f32[4,256,8,64]{1,3,2,0:T(8,128)}, f32[256,256]{1,0:T(8,128)}, /...) while((s32[]{:T(128)}, f32[4,256,8,64]{1,3,2,0:T(8,128)}, ...), condition=%wide.region_12.13_spmd, body=%wide.region_10.12_spmd.sunk | while | flops 812320768 | bytes 5482637 | solution.py:239
  493.7 4.0 multiply_reduce_fusion.4
  498.4 4.0 fusion.183
  502.5 4.0 multiply_reduce_fusion.4
  507.2 4.0 fusion.183
  511.3 4.0 multiply_reduce_fusion.4
  516.0 4.0 fusion.183
  520.1 4.0 multiply_reduce_fusion.4
  524.8 4.0 fusion.183
  530.1 3.7 fusion.105
  537.6 183.1 %all-gather.17.cloned.1.call-done = bf16[1024,64,128]{2,1,0:T(8,128)(2,1)} async-done(((bf16[32,64,128]{2,1,0:T(8,128)(2,1)}), bf16[1024,64,128]{2,1,0:T(8,128)(2,1)}) %all-gather.17.cloned.1.call-update) | async-done | bytes 16777232 | tf_op jit(solution)/shard_map/all_gather | solution.py:16
  720.8 42.2 %while.60 = (s32[]{:T(128)}, f32[32,64,128]{2,1,0:T(8,128)S(1)}, s32[]{:T(128)}, bf16[32,32]{1,0:T(8,128)(2,1)S(1)}, bf16[32,32,64,128]{3,2,1,0:T(8,128)(2,1)}, ...) while((s32[]{:T(128)}, f32[32,64,128]{2,1,0:T(8,128)S(1)}, s32[]{:T(128)}, ...), condition=%wide.region_14.15_spmd, body=%wide.region_13.14_spmd.sunk | while | flops 786470 | bytes 2621915 | solution.py:31
  763.0 4.3 fusion.99
  767.2 3.2 fusion.126
  770.4 140.8 %all-gather.19.cloned.1.call-done = bf16[1024,64,128]{2,1,0:T(8,128)(2,1)} async-done(((bf16[32,64,128]{2,1,0:T(8,128)(2,1)}), bf16[1024,64,128]{2,1,0:T(8,128)(2,1)}) %all-gather.19.cloned.1.call-update) | async-done | bytes 16777232 | tf_op jit(solution)/shard_map/all_gather | solution.py:16
  911.4 3.7 fusion.102
  919.1 8.7 convolution_bitcast_fusion
  927.9 18.7 %copy.74 = f32[2048,2304]{1,0:T(8,128)} copy(f32[2048,2304]{0,1:T(8,128)} %convolution_bitcast_fusion) | data formatting | bytes 37748736
  949.2 7.3 fusion.55
  956.5 714.1 %reduce-scatter.4.cloned.1.call-done = f32[16,2304]{1,0:T(8,128)} async-done(((f32[2048,2304]{1,0:T(8,128)}), f32[16,2304]{1,0:T(8,128)}) %reduce-scatter.4.cloned.1.call-update) | async-done | bytes 147472
  (261 shorter events, 134.3 us)
Async XLA Ops:
  7.2 73.4 %copy-start = (bf16[1,256,2048]{2,1,0:T(8,128)(2,1)S(1)}, bf16[1,256,2048]{2,1,0:T(8,128)(2,1)}, u32[]{:S(2)}) copy-start(bf16[1,256,2048]{2,1,0:T(8,128)(2,1)} %param.16) | copy-start | bytes 3145732
  7.2 0.8 copy-start.9
  7.2 73.4 %all-gather.11.cloned.1.call-start = ((), (), s32[]{:S(2)}) async-start(), calls=%async_computation.1 | async-start | bytes 11796480 | tf_op jit(solution)/shard_map/all_gather | solution.py:90
  7.9 277.4 %all-gather.15.cloned.1.call-start = ((), (), s32[]{:S(2)}) async-start(), calls=%async_computation.3 | async-start | bytes 17301504 | tf_op jit(solution)/shard_map/all_gather | solution.py:16
  9.1 77.8 %copy-start.11 = (f32[1,32,256]{1,2,0:T(8,128)}, f32[1,32,256]{1,2,0:T(8,128)S(1)}, u32[]{:S(2)}) copy-start(f32[1,32,256]{1,2,0:T(8,128)S(1)} %get-tuple-element.649) | copy-start | bytes 98308
  86.9 1.0 copy-start.8
  94.2 382.7 %all-gather.13.cloned.1.call-start = ((), (), s32[]{:S(2)}) async-start(), calls=%async_computation.2 | async-start | bytes 17301504 | tf_op jit(solution)/shard_map/all_gather | solution.py:16
  99.5 621.2 %all-gather.17.cloned.1.call-start = ((), (), s32[]{:S(2)}) async-start(), calls=%async_computation.4 | async-start | bytes 17301504 | tf_op jit(solution)/shard_map/all_gather | solution.py:16
  208.6 76.7 %copy-start.1 = (f32[4,256,8,64]{1,3,2,0:T(8,128)}, f32[4,256,8,64]{1,3,2,0:T(8,128)S(1)}, u32[]{:S(2)}) copy-start(f32[4,256,8,64]{1,3,2,0:T(8,128)S(1)} %get-tuple-element.1040) | copy-start | bytes 6291460
  477.5 2.0 copy-start.6
  479.5 2.3 copy-start.4
  484.1 1.4 copy-start.2
  488.3 423.0 %all-gather.19.cloned.1.call-start = ((), (), s32[]{:S(2)}) async-start(), calls=%async_computation.5 | async-start | bytes 17301504 | tf_op jit(solution)/shard_map/all_gather | solution.py:16
  491.8 1178.8 %reduce-scatter.4.cloned.1.call-start = ((), (), s32[]{:S(2)}) async-start(), calls=%async_computation.6 | async-start | bytes 19021824
  493.7 4.7 copy-start.14
  502.5 4.7 copy-start.14
  511.3 4.7 copy-start.14
  520.0 4.7 copy-start.14
  530.1 3.7 copy-start.3
  911.4 3.7 copy-start.5
  915.2 2.8 copy-start.10
  915.2 3.9 copy-start.12
  946.5 1.2 copy-start.7
  946.6 2.6 copy-start.13
Sparse Core Ops, SparseCore 0:
  9.7 70.8 all-gather.10
  94.3 190.9 all-gather.14
  287.5 189.3 all-gather.12
  488.4 232.2 all-gather.16
  722.2 189.0 all-gather.18
  946.7 723.8 reduce-scatter.3
where the time goes:
time: 1690 us; the launch traced here: 1680 us
  waiting for transfers between devices  1340 us (79%)
  matrix products  112 us (7%)
  other arithmetic  89.8 us (5%)
  blocking collectives  81.3 us (5%)
  local copies, waits for them, and re-layouts  39.6 us (2%)
    unnamed x7, waiting for transfers between devices  715 us
    all_gather x4, waiting for transfers between devices, entering_2(): lax.all_gather(a.astype(kind), axis)  550 us
    all_gather x1, blocking collectives, entering_2(): lax.all_gather(a.astype(kind), axis)  81.3 us
    add x62, other arithmetic, combine_states(): jnp.exp(latter[0])[:, None, None] * earlier[1] + latter[1]  80.9 us
    all_gather x1, waiting for transfers between devices, on_device(): lax.all_gather(w_in, 'fsdp', axis=0, tiled=True)  71.4 us
  transfers between devices with their start and end apart: 6, of which 6 were waited for; matrix products, arithmetic and copies ran while one was open for 11% of the time, Pallas kernels for 0%

commit v1 on v0

--- a/solution.py
+++ b/solution.py
@@ -6,6 +6,11 @@
 BLOCK = 256
 highest = lax.Precision.HIGHEST
 epsilon = 1e-05
+
+
+def gather_over(shard, mesh_axis, along):
+    outgoing = jnp.stack([shard] * lax.axis_size(mesh_axis))
+    return jnp.concatenate(lax.all_to_all(outgoing, mesh_axis, 0, 0), axis=along)
 
 
 def entering_2(shard, axis, join, neutral, backward):
@@ -86,9 +91,7 @@
     block_count = token_count // BLOCK
     per_group = 8
     projected = jnp.dot(
-        local_tokens,
-        lax.all_gather(w_in, "fsdp", axis=0, tiled=True),
-        preferred_element_type=jnp.float32,
+        local_tokens, gather_over(w_in, "fsdp", 0), preferred_element_type=jnp.float32
     )
     xbc_rows = projected.astype(jnp.bfloat16)
     xbc_rows = lax.optimization_barrier(xbc_rows)

time: 1690 us -> 1750 us (1.036)
  waiting for transfers between devices: 1340 us -> 1370 us
    all_to_all x0 -> x1, waiting for transfers between devices: none -> 105 us  [gather_over(): lax.all_to_all(outgoing, mesh_axis, 0, 0)]
    all_gather x1, waiting for transfers between devices: 71.4 us -> 0.01 us  [on_device(): lax.all_gather(w_in, 'fsdp', axis=0, tiled=True)]
    unnamed x7, waiting for transfers between devices: 715 us -> 670 us
    all_gather x4, waiting for transfers between devices: 550 us -> 593 us  [entering_2(): lax.all_gather(a.astype(kind), axis)]
  transfers between devices with their start and end apart: 6 -> 7, of which waited for: 6 -> 6; matrix products, arithmetic and copies ran while one was open for 11% -> 12% of each run, Pallas kernels for 0% -> 0%
where the time goes in v1:
time: 1750 us; the launch traced here: 1730 us
  waiting for transfers between devices  1370 us (78%)
  matrix products  111 us (6%)
  other arithmetic  90.3 us (5%)
  blocking collectives  82.9 us (5%)
  local copies, waits for them, and re-layouts  45.6 us (3%)
    unnamed x7, waiting for transfers between devices  670 us
    all_gather x4, waiting for transfers between devices, entering_2(): lax.all_gather(a.astype(kind), axis)  593 us
    all_to_all x1, waiting for transfers between devices, gather_over(): lax.all_to_all(outgoing, mesh_axis, 0, 0)  105 us
    all_gather x1, blocking collectives, entering_2(): lax.all_gather(a.astype(kind), axis)  82.9 us
    add x62, other arithmetic, combine_states(): jnp.exp(latter[0])[:, None, None] * earlier[1] + latter[1]  81.4 us
  transfers between devices with their start and end apart: 7, of which 6 were waited for; matrix products, arithmetic and copies ran while one was open for 12% of the time, Pallas kernels for 0%

profile of v1, /device:TPU:0, one launch (start us, length us, event | category | flops | bytes accessed | tf_op | source)
XLA Modules:
  0.0 1733.6 jit_solution(6493375144948769500)
XLA Ops:
  7.2 6.0 stack.2
  13.2 6.0 all-to-all-start
  20.4 104.9 %all-to-all-done = bf16[4,512,2304]{2,1,0:T(8,128)(2,1)} async-done(((bf16[4,512,2304]{2,1,0:T(8,128)(2,1)}), bf16[4,512,2304]{2,1,0:T(8,128)(2,1)}, u32[]{:S(2)}, u32[]{:S(2)}) %all-to-all-start) | async-done | bytes 9437216 | tf_op jit(solution)/shard_map/all_to_all | solution.py:13
  125.3 6.3 convolution_convert_fusion
  150.3 82.9 %all-gather = bf16[32,32,1]{1,2,0:T(2,128)(2,1)S(1)} all-gather(bf16[1,32,1]{1,2,0:T(2,128)(2,1)S(1)} %slice.83), channel_id=2, replica_groups=mesh['seq'=32,'fsdp'=4] {'seq'}, dimensions={0}, use_global_device_ids=true | all-gather | bytes 2112 | tf_op jit(solution)/shard_map/all_gather | solution.py:21
  236.6 18.4 %while.56 = (s32[]{:T(128)}, f32[4,256,8,64]{1,3,2,0:T(8,128)}, f32[4,256,8,64]{1,3,2,0:T(8,128)S(1)}, f32[256,256]{1,0:T(8,128)}, f32[4,8,256]{2,1,0:T(8,128)S(1)}, /*index=5*/f32[4,8,256]{2,1,0:T(8,128)S(1)}, s32[]{:T(128)}) while((s32[]{:T(128)}, f32[4,256,8,64]{1,3,2,0:T(8,128)}, f32[4,256,8,64]{1,3,2,0:T(8,128)S(1)}, ...), condition=%wide.region_3.4_spmd, body=%wide.region_2.3_spmd.sunk | while | flops 406063104 | bytes 2171997 | solution.py:153
  236.7 4.5 fusion.177
  241.3 4.5 fusion.177
  245.9 4.5 fusion.177
  250.5 4.5 fusion.177
  255.0 75.7 %all-gather.15.cloned.1.call-done = bf16[1024,64,128]{2,1,0:T(8,128)(2,1)} async-done(((bf16[32,64,128]{2,1,0:T(8,128)(2,1)}), bf16[1024,64,128]{2,1,0:T(8,128)(2,1)}) %all-gather.15.cloned.1.call-update) | async-done | bytes 16777232 | tf_op jit(solution)/shard_map/all_gather | solution.py:21
  330.8 42.0 %while.58 = (s32[]{:T(128)}, f32[32,64,128]{2,1,0:T(8,128)S(1)}, s32[]{:T(128)}, bf16[32,32]{1,0:T(8,128)(2,1)S(1)}, bf16[32,32,64,128]{3,2,1,0:T(8,128)(2,1)}, ...) while((s32[]{:T(128)}, f32[32,64,128]{2,1,0:T(8,128)S(1)}, s32[]{:T(128)}, bf16[32,32]{1,0:T(8,128)(2,1)S(1)}, ...), condition=%wide.region_7.8_spmd, body=%wide.region_6.7_spmd.sunk | while | flops 786470 | bytes 2621915 | solution.py:36
  372.8 148.4 %all-gather.13.cloned.1.call-done = bf16[1024,64,128]{2,1,0:T(8,128)(2,1)} async-done(((bf16[32,64,128]{2,1,0:T(8,128)(2,1)}), bf16[1024,64,128]{2,1,0:T(8,128)(2,1)}) %all-gather.13.cloned.1.call-update) | async-done | bytes 16777232 | tf_op jit(solution)/shard_map/all_gather | solution.py:21
  521.3 12.4 while.57
  550.3 35.4 %while.59 = (s32[]{:T(128)}, f32[4,256,8,64]{1,3,2,0:T(8,128)}, f32[4,256,256]{2,1,0:T(8,128)}, f32[4,256,8,64]{1,3,2,0:T(8,128)}, f32[256,256]{1,0:T(8,128)}, /...) while((s32[]{:T(128)}, f32[4,256,8,64]{1,3,2,0:T(8,128)}, ...), condition=%wide.region_12.13_spmd, body=%wide.region_10.12_spmd.sunk | while | flops 812320768 | bytes 4434033 | solution.py:242
  550.4 4.1 fusion.183
  554.5 3.9 multiply_reduce_fusion.4
  559.3 4.1 fusion.183
  563.3 3.9 multiply_reduce_fusion.4
  568.1 4.1 fusion.183
  572.2 3.9 multiply_reduce_fusion.4
  576.9 4.1 fusion.183
  581.0 3.9 multiply_reduce_fusion.4
  587.0 3.7 fusion.108
  594.5 183.1 %all-gather.19.cloned.1.call-done = bf16[1024,64,128]{2,1,0:T(8,128)(2,1)} async-done(((bf16[32,64,128]{2,1,0:T(8,128)(2,1)}), bf16[1024,64,128]{2,1,0:T(8,128)(2,1)}) %all-gather.19.cloned.1.call-update) | async-done | bytes 16777232 | tf_op jit(solution)/shard_map/all_gather | solution.py:21
  777.8 4.2 fusion.102
  782.0 185.6 %all-gather.17.cloned.1.call-done = bf16[1024,64,128]{2,1,0:T(8,128)(2,1)} async-done(((bf16[32,64,128]{2,1,0:T(8,128)(2,1)}), bf16[1024,64,128]{2,1,0:T(8,128)(2,1)}) %all-gather.17.cloned.1.call-update) | async-done | bytes 16777232 | tf_op jit(solution)/shard_map/all_gather | solution.py:21
  967.7 42.5 %while.60 = (s32[]{:T(128)}, f32[32,64,128]{2,1,0:T(8,128)S(1)}, s32[]{:T(128)}, bf16[32,32]{1,0:T(8,128)(2,1)S(1)}, bf16[32,32,64,128]{3,2,1,0:T(8,128)(2,1)}, ...) while((s32[]{:T(128)}, f32[32,64,128]{2,1,0:T(8,128)S(1)}, s32[]{:T(128)}, ...), condition=%wide.region_14.15_spmd, body=%wide.region_13.14_spmd.sunk | while | flops 786470 | bytes 2621915 | solution.py:36
  1019.0 8.8 convolution_bitcast_fusion
  1027.8 18.7 %copy.74 = f32[2048,2304]{1,0:T(8,128)} copy(f32[2048,2304]{0,1:T(8,128)} %convolution_bitcast_fusion) | data formatting | bytes 37748736
  1049.1 7.4 fusion.55
  1056.6 669.8 %reduce-scatter.4.cloned.1.call-done = f32[16,2304]{1,0:T(8,128)} async-done(((f32[2048,2304]{1,0:T(8,128)}), f32[16,2304]{1,0:T(8,128)}) %reduce-scatter.4.cloned.1.call-update) | async-done | bytes 147472
  (258 shorter events, 142.3 us)
Async XLA Ops:
  7.2 118.1 %copy-start = (bf16[1,256,2048]{2,1,0:T(8,128)(2,1)S(1)}, bf16[1,256,2048]{2,1,0:T(8,128)(2,1)}, u32[]{:S(2)}) copy-start(bf16[1,256,2048]{2,1,0:T(8,128)(2,1)} %param.16) | copy-start | bytes 3145732
  13.2 6.0 copy-start.9
  13.2 112.1 %all-to-all-start = ((bf16[4,512,2304]{2,1,0:T(8,128)(2,1)}), bf16[4,512,2304]{2,1,0:T(8,128)(2,1)}, u32[]{:S(2)}, u32[]{:S(2)}) async-start(bf16[4,512,2304]{2,1,0:T(8,128)(2,1)} %stack.2), calls=%async_computation | async-start | bytes 18874368 | tf_op jit(solution)/shard_map/all_to_all | solution.py:13
  19.2 311.5 %all-gather.15.cloned.1.call-start = ((), (), s32[]{:S(2)}) async-start(), calls=%async_computation.4 | async-start | bytes 17301504 | tf_op jit(solution)/shard_map/all_gather | solution.py:21
  20.3 111.2 %copy-start.11 = (f32[1,32,256]{1,2,0:T(8,128)}, f32[1,32,256]{1,2,0:T(8,128)S(1)}, u32[]{:S(2)}) copy-start(f32[1,32,256]{1,2,0:T(8,128)S(1)} %get-tuple-element.649) | copy-start | bytes 98308
  131.5 1.1 copy-start.8
  138.9 382.3 %all-gather.13.cloned.1.call-start = ((), (), s32[]{:S(2)}) async-start(), calls=%async_computation.3 | async-start | bytes 17301504 | tf_op jit(solution)/shard_map/all_gather | solution.py:21
  144.2 633.5 %all-gather.19.cloned.1.call-start = ((), (), s32[]{:S(2)}) async-start(), calls=%async_computation.6 | async-start | bytes 17301504 | tf_op jit(solution)/shard_map/all_gather | solution.py:21
  255.0 75.8 %copy-start.1 = (f32[4,256,8,64]{1,3,2,0:T(8,128)}, f32[4,256,8,64]{1,3,2,0:T(8,128)S(1)}, u32[]{:S(2)}) copy-start(f32[4,256,8,64]{1,3,2,0:T(8,128)S(1)} %get-tuple-element.1040) | copy-start | bytes 6291460
  533.8 2.0 copy-start.6
  535.8 2.3 copy-start.4
  540.4 1.4 copy-start.2
  544.5 423.0 %all-gather.17.cloned.1.call-start = ((), (), s32[]{:S(2)}) async-start(), calls=%async_computation.5 | async-start | bytes 17301504 | tf_op jit(solution)/shard_map/all_gather | solution.py:21
  548.1 501.0 %all-gather.11.cloned.1.call-start = ((), (), s32[]{:S(2)}) async-start(), calls=%async_computation.2 | async-start | bytes 11796480 | tf_op jit(solution)/shard_map/all_gather | solution.py:310
  548.7 1177.7 %reduce-scatter.4.cloned.1.call-start = ((), (), s32[]{:S(2)}) async-start(), calls=%async_computation.7 | async-start | bytes 19021824
  587.0 3.7 copy-start.3
  1010.2 3.6 copy-start.10
  1013.9 3.2 copy-start.5
  1015.1 3.9 copy-start.13
  1017.0 2.0 copy-start.12
  1046.5 1.2 copy-start.7
  1046.5 2.6 copy-start.14
Sparse Core Ops, SparseCore 0:
  139.0 191.6 all-gather.14
  332.9 188.2 all-gather.12
  544.7 232.9 all-gather.18
  779.1 188.4 all-gather.16
  969.1 66.9 all-gather.10
  1046.6 679.6 reduce-scatter.3
